TPU v7x, 256 devices: a whole 4x4x8 slice. The times are simulated.
256 devices in a mesh: tm: 16 (over x, z_hi, core), input: 16 (over z_lo, y).
Axes of the slice: x: 4, y: 4, z: 8 (z_hi: 2, z_lo: 4; z = z_hi * 4 + z_lo), core: 2. Of those that a mesh axis runs over, the one named last changes fastest.
Arguments:
- samples: bfloat16 [2, 262144, 2048], P(None, 'tm', 'input'), may hold values from -6 to 6
- filter_taps: float32 [16, 1024], replicated, may hold values from -1.5 to 1.5
Outputs:
- visibilities: bfloat16 [2, 64, 2048, 2048], P(None, 'tm', 'input')
All inputs are finite; a program needn't handle non-finite values.
Results may differ from a plain program's by a relative error of at most 0.0056.
Values may be sent and summed in bfloat16 or wider, within the bound.
A program may use at most 192 MiB of HBM per device.

v0:
```python
import jax
import jax.numpy as jnp
from jax import lax
from jax.sharding import PartitionSpec as P

CH_DEV = 4


def passed_along(shard, axis, by):
    size = lax.axis_size(axis)
    pairs = [(i, i + by) for i in range(size) if 0 <= i + by < size]
    return lax.ppermute(shard, axis, pairs)


def dft_table(count, length):
    chan = jnp.arange(count, dtype=jnp.int32)
    point = jnp.arange(length, dtype=jnp.int32)
    phase = chan[:, None] * point[None, :] % length
    theta = 2.0 * jnp.pi / length * phase.astype(jnp.float32)
    scale = 1.0 / jnp.sqrt(jnp.float32(length))
    cosine = jnp.cos(theta) * scale
    sine = jnp.sin(theta) * scale
    real_rows = jnp.stack([cosine, sine], axis=1)
    imag_rows = jnp.stack([-sine, cosine], axis=1)
    return jnp.concatenate([real_rows, imag_rows], axis=0)


def filter_frames(padded, filter_taps, count):
    filtered = jnp.zeros((2, count, padded.shape[2], padded.shape[3]), jnp.float32)
    for tap in range(filter_taps.shape[0]):
        filtered = filtered + filter_taps[tap][None, None, :, None] * padded[
            :, tap : tap + count
        ].astype(jnp.float32)
    return filtered


def transform(filtered, table):
    spectra = jnp.einsum("kcn,cfna->kfa", table, filtered, precision=lax.Precision.HIGHEST)
    return spectra.reshape(2, table.shape[0] // 2, filtered.shape[1], filtered.shape[3])


def on_device(samples, filter_taps):
    nch = filter_taps.shape[1]
    rim = filter_taps.shape[0] - 1
    width = samples.shape[2]
    frames_here = samples.shape[1] // nch
    local = samples.reshape(2, frames_here, nch, width)
    table = dft_table(CH_DEV * lax.axis_size("tm"), nch)
    ahead = passed_along(local[:, :rim], "tm", -1)
    padded = jnp.concatenate([local, ahead], axis=1)
    spectra = transform(filter_frames(padded, filter_taps, frames_here), table)
    spectra = spectra.astype(jnp.bfloat16)
    turned = lax.all_to_all(spectra, "tm", split_axis=1, concat_axis=2, tiled=True)
    scale = 1.0 / turned.shape[2]
    real_part = turned[0]
    imag_part = turned[1]
    left = jnp.concatenate(
        [
            jnp.concatenate([real_part, imag_part], axis=1),
            jnp.concatenate([imag_part, -real_part], axis=1),
        ],
        axis=2,
    )
    right_block = lax.all_gather(turned, "input", axis=3, tiled=True)
    stacked = jnp.concatenate([right_block[0], right_block[1]], axis=1)
    product = jnp.einsum("cfa,cfb->cab", left, stacked, preferred_element_type=jnp.float32) * scale
    product = product.reshape(product.shape[0], 2, width, right_block.shape[3])
    return jnp.transpose(product, (1, 0, 2, 3)).astype(jnp.bfloat16)


def solution(mesh):
    in_specs = (P(None, "tm", "input"), P())
    out_specs = P(None, "tm", "input", None)
    return jax.shard_map(
        on_device, mesh=mesh, in_specs=in_specs, out_specs=out_specs, check_vma=False
    )
```

profile of v0, /device:TPU:8, one launch (start us, length us, event | category | flops | bytes accessed | tf_op | source)
XLA Modules:
  0.0 424.8 jit_solution(3179844550799687338)
XLA Ops:
  6.5 0.0 copy-start
  6.5 0.0 all-gather.2.cloned.1.call-start
  6.5 4.1 slice.146
  10.6 4.0 copy.51
  14.6 1.3 collective-permute-start
  15.9 1.0 fusion.110
  16.9 1.0 sine_multiply_fusion
  17.9 0.0 copy-done
  18.0 7.5 %constant_dynamic-update-slice_fusion.1 = bf16[2,31,1024,128]{3,2,0,1:T(8,128)(2,1)} fusion(bf16[2,16,1024,128]{3,2,1,0:T(8,128)(2,1)} %bitcast.48), kind=kLoop, calls=%fused_computation.116 | loop fusion | bytes 16777216
  25.5 3.7 collective-permute-done
  29.2 7.1 %constant_dynamic-update-slice_fusion = bf16[2,31,1024,128]{3,2,0,1:T(8,128)(2,1)} fusion(bf16[2,31,1024,128]{3,2,0,1:T(8,128)(2,1)} %constant_dynamic-update-slice_fusion.1, bf16[2,15,1024,128]{3,2,0,1:T(8,128)(2,1)} %collective-permute-done), kind=kLoop, calls=%fused_computation.115 | loop fusion | bytes 15728640 | tf_op jit(solution)/shard_map/concatenate | solution.py:50
  36.4 46.7 %fusion.119 = f32[2,16,1024,128]{3,2,0,1:T(8,128)S(1)} fusion(bf16[2,31,1024,128]{3,2,0,1:T(8,128)(2,1)} %constant_dynamic-update-slice_fusion, f32[1024]{0:T(1024)S(1)} %bitcast.71, f32[1024]{0:T(1024)S(1)} %bitcast.72, f32[1024]{0:T(1024)S(1)} %bitcast.58, f32[1024]{0:T(1024)S(1)} %bitcast.59, f32[1024]{0:T(1024)S(1)} %bitcast.60, ...), kind=kLoop, calls=%fused_computation.1.clone.clone.clone.clone.clone.2 | loop fusion | flops 197132288 | bytes 151060480 | tf_op jit(solution)/shard_map/kcn,cfna->kfa/dot_general | solution.py:38
  83.1 8.9 %fusion.88 = bf16[128,16,128]{2,0,1:T(8,128)(2,1)S(1)} fusion(f32[64,1,1024]{2,0,1:T(8,128)S(1)} %get-tuple-element.26, f32[64,1,1024]{2,0,1:T(8,128)S(1)} %fusion.110, f32[64,1,1024]{2,0,1:T(8,128)S(1)} %get-tuple-element.25, f32[2,16,1024,128]{3,2,0,1:T(8,128)S(1)} %fusion.119), kind=kOutput, calls=%fused_computation.88 | convolution fusion | flops 6443499520 | bytes 18087936 | tf_op jit(solution)/shard_map/kcn,cfna->kfa/dot_general | solution.py:38
  92.0 0.3 copy.33
  92.3 192.0 %all_to_all.18 = bf16[2,64,16,128]{3,2,0,1:T(8,128)(2,1)S(1)} all-to-all(bf16[2,64,16,128]{3,2,0,1:T(8,128)(2,1)S(1)} %copy.33), channel_id=1, replica_groups=mesh['tm'=16,'input'=16] {'tm'}, dimensions={1} | all-to-all | bytes 1048576 | tf_op jit(solution)/shard_map/all_to_all | solution.py:53
  284.3 0.8 copy.41
  285.1 0.0 all-gather.2.cloned.1.call-update
  285.3 0.1 copy.37
  285.5 0.1 copy.38
  285.7 123.6 %all-gather.2.cloned.1.call-done = bf16[2,4,256,2048]{3,2,1,0:T(8,128)(2,1)} async-done(((bf16[2,4,256,128]{3,2,1,0:T(8,128)(2,1)}), bf16[2,4,256,2048]{3,2,1,0:T(8,128)(2,1)}) %all-gather.2.cloned.1.call-update) | async-done | bytes 8388624 | tf_op jit(solution)/shard_map/all_gather | solution.py:64
  409.2 3.8 slice_bitcast_fusion.1
  413.0 2.6 multiply_convert_fusion
  415.7 2.3 copy.56
  (6 shorter events, 0.2 us)
Async XLA Ops:
  6.5 11.4 %copy-start = (f32[16,1024]{1,0:T(8,128)S(1)}, f32[16,1024]{1,0:T(8,128)}, u32[]{:S(2)}) copy-start(f32[16,1024]{1,0:T(8,128)} %param.3) | copy-start | bytes 196612
  6.5 402.7 %all-gather.2.cloned.1.call-start = ((), (), s32[]{:S(2)}) async-start(), calls=%async_computation.1 | async-start | bytes 8912896 | tf_op jit(solution)/shard_map/all_gather | solution.py:64
  14.6 14.6 %collective-permute-start = (bf16[2,15,1024,128]{3,2,0,1:T(8,128)(2,1)}, bf16[2,15,1024,128]{3,2,0,1:T(8,128)(2,1)}, u32[]{:S(2)}, u32[]{:S(2)}) collective-permute-start(bf16[2,15,1024,128]{3,2,0,1:T(8,128)(2,1)} %copy.51), channel_id=1, source_target_pairs={{16,0},{32,16},{48,32},{64,48},{80,64},{96,80},{112,96},{128,112},... | collective-permute-start | bytes 23592968 | tf_op jit(solution)/shard_map/ppermute | solution.py:12
Sparse Core Ops, SparseCore 0:
  285.3 123.9 all-gather.1
where the time goes:
time: 425 us
  blocking collectives  192 us (45%)
  waiting for transfers between devices  127 us (30%)
  other arithmetic  48.8 us (11%)
  local copies, waits for them, and re-layouts  30.4 us (7%)
  between operations  13.5 us (3%)
  matrix products  11.5 us (3%)
    all_to_all x1, blocking collectives, on_device(): lax.all_to_all(spectra, 'tm', split_axis=1, concat_axis=2, tiled=True)  192 us
    all_gather x1, waiting for transfers between devices, on_device(): right_block = lax.all_gather(turned, 'input', axis=3, tiled=True)  124 us
    dot_general x1, other arithmetic, transform(): jnp.einsum('kcn,cfna->kfa', table, filtered, precision=lax.Precision.HIGH...  46.7 us
    unnamed x4, local copies, waits for them, and re-layouts  11.5 us
    dot_general x1, matrix products, transform(): jnp.einsum('kcn,cfna->kfa', table, filtered, precision=lax.Precision.HIGH...  8.89 us
  transfers between devices with their start and end apart: 2, of which 2 were waited for; matrix products, arithmetic and copies ran while one was open for 2% of the time, Pallas kernels for 0%

commit v1 on v0

--- a/solution.py
+++ b/solution.py
@@ -61,7 +61,9 @@
         ],
         axis=2,
     )
-    right_block = lax.all_gather(turned, "input", axis=3, tiled=True)
+    right_block = jnp.concatenate(
+        lax.all_to_all(jnp.stack([turned] * lax.axis_size("input")), "input", 0, 0), axis=3
+    )
     stacked = jnp.concatenate([right_block[0], right_block[1]], axis=1)
     product = jnp.einsum("cfa,cfb->cab", left, stacked, preferred_element_type=jnp.float32) * scale
     product = product.reshape(product.shape[0], 2, width, right_block.shape[3])

time: 425 us -> 512 us (1.20)
  the two profiles are of different devices: /device:TPU:8 before, /device:TPU:64 now
where the time goes in v1:
time: 512 us
  blocking collectives  192 us (38%)
  waiting for transfers between devices  186 us (36%)
  local copies, waits for them, and re-layouts  62.4 us (12%)
  other arithmetic  49.1 us (10%)
  matrix products  13.7 us (3%)
  starting transfers between devices  8.13 us (2%)
    all_to_all x1, blocking collectives, on_device(): lax.all_to_all(spectra, 'tm', split_axis=1, concat_axis=2, tiled=True)  192 us
    all_to_all x1, waiting for transfers between devices, on_device(): lax.all_to_all(jnp.stack([turned] * lax.axis_size('input')), 'input', 0, 0)  182 us
    dot_general x1, other arithmetic, transform(): jnp.einsum('kcn,cfna->kfa', table, filtered, precision=lax.Precision.HIGH...  47.1 us
    slice x3, local copies, waits for them, and re-layouts, on_device(): stacked = jnp.concatenate([right_block[0], right_block[1]], axis=1)  16.7 us
    squeeze x2, local copies, waits for them, and re-layouts, on_device(): stacked = jnp.concatenate([right_block[0], right_block[1]], axis=1)  14.6 us
    unnamed x4, local copies, waits for them, and re-layouts  11.5 us
  transfers between devices with their start and end apart: 2, of which 2 were waited for; matrix products, arithmetic and copies ran while one was open for 2% of the time, Pallas kernels for 0%

profile of v1, /device:TPU:64, one launch (start us, length us, event | category | flops | bytes accessed | tf_op | source)
XLA Modules:
  0.0 511.6 jit_solution(9369154438631796447)
XLA Ops:
  0.0 0.0 copy-start
  0.0 4.1 slice.148
  4.1 4.0 copy.52
  8.1 1.3 collective-permute-start
  9.3 1.0 fusion.110
  10.3 1.0 sine_multiply_fusion
  11.4 0.0 copy-done
  11.4 7.5 %constant_dynamic-update-slice_fusion.1 = bf16[2,31,1024,128]{3,2,0,1:T(8,128)(2,1)} fusion(bf16[2,16,1024,128]{3,2,1,0:T(8,128)(2,1)} %bitcast.49), kind=kLoop, calls=%fused_computation.114 | loop fusion | bytes 16777216
  19.0 3.7 collective-permute-done
  22.7 7.1 %constant_dynamic-update-slice_fusion = bf16[2,31,1024,128]{3,2,0,1:T(8,128)(2,1)} fusion(bf16[2,31,1024,128]{3,2,0,1:T(8,128)(2,1)} %constant_dynamic-update-slice_fusion.1, bf16[2,15,1024,128]{3,2,0,1:T(8,128)(2,1)} %collective-permute-done), kind=kLoop, calls=%fused_computation.113 | loop fusion | bytes 15728640 | tf_op jit(solution)/shard_map/concatenate | solution.py:50
  29.8 47.1 %fusion.120 = f32[2,16,1024,128]{3,2,0,1:T(8,128)S(1)} fusion(bf16[2,31,1024,128]{3,2,0,1:T(8,128)(2,1)} %constant_dynamic-update-slice_fusion, f32[1024]{0:T(1024)S(1)} %bitcast.72, f32[1024]{0:T(1024)S(1)} %bitcast.73, f32[1024]{0:T(1024)S(1)} %bitcast.59, f32[1024]{0:T(1024)S(1)} %bitcast.60, f32[1024]{0:T(1024)S(1)} %bitcast.61, ...), kind=kLoop, calls=%fused_computation.1.clone.clone.clone.clone.clone.2 | loop fusion | flops 197132288 | bytes 151060480 | tf_op jit(solution)/shard_map/kcn,cfna->kfa/dot_general | solution.py:38
  76.9 8.9 %fusion.88 = bf16[128,16,128]{2,0,1:T(8,128)(2,1)S(1)} fusion(f32[64,1,1024]{2,0,1:T(8,128)S(1)} %get-tuple-element.26, f32[64,1,1024]{2,0,1:T(8,128)S(1)} %fusion.110, f32[64,1,1024]{2,0,1:T(8,128)S(1)} %get-tuple-element.25, f32[2,16,1024,128]{3,2,0,1:T(8,128)S(1)} %fusion.120), kind=kOutput, calls=%fused_computation.86 | convolution fusion | flops 6443499520 | bytes 18087936 | tf_op jit(solution)/shard_map/kcn,cfna->kfa/dot_general | solution.py:38
  85.8 0.3 copy.32
  86.1 192.2 %all_to_all.20 = bf16[2,64,16,128]{3,2,0,1:T(8,128)(2,1)S(1)} all-to-all(bf16[2,64,16,128]{3,2,0,1:T(8,128)(2,1)S(1)} %copy.32), channel_id=1, replica_groups=mesh['tm'=16,'input'=16] {'tm'}, dimensions={1} | all-to-all | bytes 1048576 | tf_op jit(solution)/shard_map/all_to_all | solution.py:53
  278.4 5.3 %stack.11 = bf16[16,2,4,256,128]{4,3,2,1,0:T(8,128)(2,1)} broadcast(bf16[2,4,256,128]{3,2,1,0:T(8,128)(2,1)S(1)} %bitcast.54), dimensions={1,2,3,4} | broadcast | bytes 8912896 | tf_op jit(solution)/shard_map/stack | solution.py:65
  283.7 6.8 %all-to-all-start.1 = ((bf16[16,2,4,256,128]{4,3,2,1,0:T(8,128)(2,1)}), bf16[16,2,4,256,128]{4,3,2,1,0:T(8,128)(2,1)}, u32[]{:S(2)}, u32[]{:S(2)}) async-start(bf16[16,2,4,256,128]{4,3,2,1,0:T(8,128)(2,1)} %stack.11), calls=%async_computation.1 | async-start | bytes 16777216 | tf_op jit(solution)/shard_map/all_to_all | solution.py:65
  290.6 0.1 copy.36
  290.9 0.1 copy.37
  291.0 182.2 %all-to-all-done.1 = bf16[16,2,4,256,128]{4,3,2,1,0:T(8,128)(2,1)} async-done(((bf16[16,2,4,256,128]{4,3,2,1,0:T(8,128)(2,1)}), bf16[16,2,4,256,128]{4,3,2,1,0:T(8,128)(2,1)}, u32[]{:S(2)}, u32[]{:S(2)}) %all-to-all-start.1) | async-done | bytes 8388640 | tf_op jit(solution)/shard_map/all_to_all | solution.py:65
  473.2 5.2 %fusion.114 = (bf16[1,4,256,16,128]{4,2,1,0,3:T(8,128)(2,1)S(1)}, bf16[1,4,256,16,128]{4,2,1,0,3:T(8,128)(2,1)}) fusion(bf16[2,4,256,16,128]{4,2,1,0,3:T(8,128)(2,1)} %bitcast.28), kind=kLoop, calls=%fused_computation.118 | loop fusion | bytes 16777216 | tf_op jit(solution)/shard_map/slice | solution.py:67
  478.4 4.7 copy.41
  483.1 7.3 %squeeze.14 = bf16[4,256,2048]{2,1,0:T(8,128)(2,1)} reshape(bf16[1,4,256,16,128]{4,3,2,1,0:T(8,128)(2,1)} %copy.41) | data formatting | bytes 8388608 | tf_op jit(solution)/shard_map/squeeze | solution.py:67
  490.4 6.9 %copy.42 = bf16[1,4,256,16,128]{4,3,2,1,0:T(8,128)(2,1)} copy(bf16[1,4,256,16,128]{4,2,1,0,3:T(8,128)(2,1)} %get-tuple-element.6) | data formatting | bytes 8388608 | tf_op jit(solution)/shard_map/slice | solution.py:67
  497.2 7.3 %squeeze.15 = bf16[4,256,2048]{2,1,0:T(8,128)(2,1)} reshape(bf16[1,4,256,16,128]{4,3,2,1,0:T(8,128)(2,1)} %copy.42) | data formatting | bytes 8388608 | tf_op jit(solution)/shard_map/squeeze | solution.py:67
  504.5 4.8 multiply_convert_fusion
  509.3 2.3 copy.57
  (7 shorter events, 0.2 us)
Async XLA Ops:
  0.0 11.4 %copy-start = (f32[16,1024]{1,0:T(8,128)S(1)}, f32[16,1024]{1,0:T(8,128)}, u32[]{:S(2)}) copy-start(f32[16,1024]{1,0:T(8,128)} %param.3) | copy-start | bytes 196612
  8.1 14.6 %collective-permute-start = (bf16[2,15,1024,128]{3,2,0,1:T(8,128)(2,1)}, bf16[2,15,1024,128]{3,2,0,1:T(8,128)(2,1)}, u32[]{:S(2)}, u32[]{:S(2)}) collective-permute-start(bf16[2,15,1024,128]{3,2,0,1:T(8,128)(2,1)} %copy.52), channel_id=1, source_target_pairs={{16,0},{32,16},{48,32},{64,48},{80,64},{96,80},{112,96},{128,112},... | collective-permute-start | bytes 23592968 | tf_op jit(solution)/shard_map/ppermute | solution.py:12
  283.7 189.6 %all-to-all-start.1 = ((bf16[16,2,4,256,128]{4,3,2,1,0:T(8,128)(2,1)}), bf16[16,2,4,256,128]{4,3,2,1,0:T(8,128)(2,1)}, u32[]{:S(2)}, u32[]{:S(2)}) async-start(bf16[16,2,4,256,128]{4,3,2,1,0:T(8,128)(2,1)} %stack.11), calls=%async_computation.1 | async-start | bytes 16777216 | tf_op jit(solution)/shard_map/all_to_all | solution.py:65
